TPU v7x, 512 devices: a whole 4x8x8 slice. The times are simulated.
512 devices in a mesh: gx: 4 (over x), rest: 128 (over y, z, core).
Axes of the slice: x: 4, y: 8, z: 8, core: 2. Of those that a mesh axis runs over, the one named last changes fastest.
Arguments:
- tensor: float32 [512, 672, 672], P('rest', 'gx'), as said below
- basis: float32 [672, 128], P('gx'), may hold values from -0.25 to 0.25
Outputs:
- gram_one: float32 [672, 672], P('gx')
- core: float32 [128, 512, 672], P('gx', 'rest')
- gram_two: float32 [672, 672], replicated
Inputs may be any that keep to these rules, and one draw needn't show every extreme that they name: `tensor`: Real-valued field samples.
All inputs are finite; a program needn't handle non-finite values.
Results may differ from a plain program's by a relative error of at most 0.000073.
Values sent between devices are 32-bit elements; how exact they have to be, the bound alone decides.
No kernel may reach another device: no remote copies, remote signals or barrier semaphores. Data moves between devices by JAX's collectives and lax.ppermute only.
A program may use at most 64 MiB of HBM per device.

v0:
```python
import jax
import jax.numpy as jnp
from jax import lax
from jax.sharding import PartitionSpec as P


def local(tensor, basis):
    highest = lax.Precision.HIGHEST
    slices_here = tensor.shape[0]
    rows_here = tensor.shape[1]
    second_width = tensor.shape[2]
    slices_all = slices_here * lax.axis_size("rest")
    rank_all = basis.shape[1]
    exchanged = lax.all_to_all(tensor, "gx", split_axis=2, concat_axis=1, tiled=True)
    local_gram = jnp.einsum("kic,kjc->ij", exchanged, exchanged, precision=highest)
    summed = lax.psum(local_gram, ("gx", "rest"))
    block_rows = lax.dynamic_slice_in_dim(summed, lax.axis_index("gx") * rows_here, rows_here, 0)
    gram_one = block_rows / (slices_all * second_width)
    core = lax.psum_scatter(
        jnp.einsum("ic,kij->ckj", basis, tensor, precision=highest),
        "gx",
        scatter_dimension=0,
        tiled=True,
    )
    core_flat = core.reshape(-1, second_width)
    local_two = jnp.dot(
        core_flat.T, core_flat, precision=highest, preferred_element_type=jnp.float32
    )
    gram_sum = lax.psum(local_two, ("gx", "rest"))
    gram_two = gram_sum / (slices_all * rank_all)
    return (gram_one, core, gram_two)


def solution(mesh):
    in_specs = (P("rest", "gx", None), P("gx", None))
    out_specs = (P("gx", None), P("gx", "rest", None), P())
    return jax.shard_map(local, mesh=mesh, in_specs=in_specs, out_specs=out_specs, check_vma=False)
```

profile of v0, /device:TPU:24, one launch (start us, length us, event | category | flops | bytes accessed | tf_op | source)
XLA Modules:
  0.0 385.6 jit_solution(14953553316876162083)
XLA Ops:
  7.2 0.0 copy-start
  7.2 0.0 reduce-scatter.2.cloned.1.call-start
  7.2 0.8 copy-done
  8.1 4.3 %fusion = f32[128,4,672]{2,0,1:T(8,128)} fusion(f32[4,168,672]{2,1,0:T(8,128)} %param.2, f32[168,128]{1,0:T(8,128)S(1)} %copy-done), kind=kOutput, calls=%fused_computation.5 | convolution fusion | flops 693633024 | bytes 3268608 | tf_op jit(solution)/shard_map/ic,kij->ckj/dot_general | solution.py:20
  12.3 0.0 reduce-scatter.2.cloned.1.call-update
  12.3 0.0 all-reduce.3.cloned.1.call-start
  12.4 3.2 copy.7
  15.6 50.1 %all_to_all.18 = f32[4,168,672]{1,0,2:T(4,128)S(1)} all-to-all(f32[4,168,672]{1,0,2:T(4,128)S(1)} %copy.7), channel_id=1, replica_groups=mesh['gx'=4,'rest'=128] {'gx'}, dimensions={2} | all-to-all | bytes 3612672 | tf_op jit(solution)/shard_map/all_to_all | solution.py:14
  65.7 1.8 copy.11
  67.4 2.9 all_to_all.16
  70.3 8.9 %convolution_bitcast_fusion.1 = f32[672,672]{1,0:T(8,128)} fusion(f32[4,672,168]{1,2,0:T(8,128)} %all_to_all.16), kind=kOutput, calls=%fused_computation.2 | convolution fusion | flops 3641573376 | bytes 3612672 | tf_op jit(solution)/shard_map/kic,kjc->ij/dot_general | solution.py:15
  79.2 0.0 reduce-scatter.2.cloned.1.call-done
  79.2 4.2 %convolution_bitcast_fusion = f32[672,672]{1,0:T(8,128)} fusion(f32[32,4,672]{2,0,1:T(8,128)} %reduce-scatter.2.cloned.1.call-done), kind=kOutput, calls=%fused_computation.1 | convolution fusion | flops 693633024 | bytes 2150400 | tf_op jit(solution)/shard_map/dot_general | solution.py:26
  83.4 0.0 copy-start.1
  83.4 0.0 all-reduce.3.cloned.1.call-update
  83.5 1.0 copy-done.1
  84.4 1.0 copy.9
  85.4 288.4 %all-reduce.3.cloned.1.call-done = (f32[672,672]{1,0:T(8,128)}, f32[672,672]{1,0:T(8,128)}) async-done(((f32[672,672]{1,0:T(8,128)}, f32[672,672]{1,0:T(8,128)}), (f32[672,672]{1,0:T(8,128)}, f32[672,672]{1,0:T(8,128)})) %all-reduce.3.cloned.1.call-update) | async-done | bytes 3612688 | tf_op jit(solution)/shard_map/psum | solution.py:16
  373.9 3.0 broadcast_multiply_fusion
  376.9 1.9 dynamic-slice_multiply_fusion
Async XLA Ops:
  7.2 0.9 copy-start
  7.2 72.0 %reduce-scatter.2.cloned.1.call-start = ((), (), s32[]{:S(2)}) async-start(), calls=%async_computation.2 | async-start | bytes 1966080 | tf_op jit(solution)/shard_map/reduce_scatter | solution.py:19
  12.3 361.5 %all-reduce.3.cloned.1.call-start = ((), (), s32[]{:S(2)}) async-start(), calls=%async_computation.3 | async-start | bytes 8257536 | tf_op jit(solution)/shard_map/psum | solution.py:16
  83.4 1.0 copy-start.1
Sparse Core Ops, SparseCore 0:
  12.5 53.5 reduce-scatter.1
  83.6 290.2 all-reduce.2
where the time goes:
time: 386 us
  waiting for transfers between devices  288 us (75%)
  blocking collectives  50.1 us (13%)
  matrix products  17.4 us (5%)
  between operations  14.1 us (4%)
  local copies, waits for them, and re-layouts  10.7 us (3%)
  other arithmetic  4.89 us (1%)
    psum x1, waiting for transfers between devices, local(): summed = lax.psum(local_gram, ('gx', 'rest'))  288 us
    all_to_all x1, blocking collectives, local(): lax.all_to_all(tensor, 'gx', split_axis=2, concat_axis=1, tiled=True)  50.1 us
    dot_general x1, matrix products, local(): jnp.einsum('kic,kjc->ij', exchanged, exchanged, precision=highest)  8.86 us
  transfers between devices with their start and end apart: 2, of which 1 were waited for; matrix products, arithmetic and copies ran while one was open for 4% of the time, Pallas kernels for 0%

commit v1 on v0

--- a/solution.py
+++ b/solution.py
@@ -13,7 +13,8 @@
     rank_all = basis.shape[1]
     exchanged = lax.all_to_all(tensor, "gx", split_axis=2, concat_axis=1, tiled=True)
     local_gram = jnp.einsum("kic,kjc->ij", exchanged, exchanged, precision=highest)
-    summed = lax.psum(local_gram, ("gx", "rest"))
+    partial = lax.psum(local_gram, "rest")
+    summed = lax.psum(partial, "gx")
     block_rows = lax.dynamic_slice_in_dim(summed, lax.axis_index("gx") * rows_here, rows_here, 0)
     gram_one = block_rows / (slices_all * second_width)
     core = lax.psum_scatter(

time: 386 us -> 643 us (1.67)
  the two profiles are of different devices: /device:TPU:24 before, /device:TPU:1 now
where the time goes in v1:
time: 643 us
  waiting for transfers between devices  549 us (85%)
  blocking collectives  45.6 us (7%)
  matrix products  17.4 us (3%)
  between operations  15.7 us (2%)
  local copies, waits for them, and re-layouts  9.71 us (2%)
    psum x1, waiting for transfers between devices, local(): gram_sum = lax.psum(local_two, ('gx', 'rest'))  281 us
    psum x1, waiting for transfers between devices, local(): partial = lax.psum(local_gram, 'rest')  204 us
    psum x1, waiting for transfers between devices, local(): summed = lax.psum(partial, 'gx')  64.6 us
    all_to_all x1, blocking collectives, local(): lax.all_to_all(tensor, 'gx', split_axis=2, concat_axis=1, tiled=True)  45.6 us
  transfers between devices with their start and end apart: 4, of which 3 were waited for; matrix products, arithmetic and copies ran while one was open for 3% of the time, Pallas kernels for 0%

profile of v1, /device:TPU:1, one launch (start us, length us, event | category | flops | bytes accessed | tf_op | source)
XLA Modules:
  0.0 642.9 jit_solution(414020160427256137)
XLA Ops:
  8.0 0.0 copy-start
  8.0 0.0 reduce-scatter.2.cloned.1.call-start
  8.1 0.8 copy-done
  8.9 4.3 fusion
  13.2 0.0 reduce-scatter.2.cloned.1.call-update
  13.2 0.0 all-reduce.4.cloned.1.call-start
  13.2 3.2 copy.7
  16.4 45.6 %all_to_all.18 = f32[4,168,672]{1,0,2:T(4,128)S(1)} all-to-all(f32[4,168,672]{1,0,2:T(4,128)S(1)} %copy.7), channel_id=1, replica_groups=mesh['gx'=4,'rest'=128] {'gx'}, dimensions={2} | all-to-all | bytes 3612672 | tf_op jit(solution)/shard_map/all_to_all | solution.py:14
  62.1 1.8 copy.11
  63.8 2.9 all_to_all.16
  66.7 8.8 %convolution_bitcast_fusion.1 = f32[672,672]{1,0:T(8,128)} fusion(f32[4,672,168]{1,2,0:T(8,128)} %all_to_all.16), kind=kOutput, calls=%fused_computation.2 | convolution fusion | flops 3641573376 | bytes 3612672 | tf_op jit(solution)/shard_map/kic,kjc->ij/dot_general | solution.py:15
  75.6 0.0 all-reduce.4.cloned.1.call-update
  75.6 0.2 all-reduce.8.cloned.1.call-start
  75.8 0.0 reduce-scatter.2.cloned.1.call-done
  75.9 4.3 convolution_bitcast_fusion
  80.1 0.0 copy-start.1
  80.1 0.0 all-reduce.8.cloned.1.call-update
  80.2 0.0 all-reduce.6.cloned.1.call-start
  80.2 203.6 %all-reduce.4.cloned.1.call-done = f32[672,672]{1,0:T(8,128)} async-done(((f32[672,672]{1,0:T(8,128)}), f32[672,672]{1,0:T(8,128)}) %all-reduce.4.cloned.1.call-update) | async-done | bytes 1806352 | tf_op jit(solution)/shard_map/psum | solution.py:16
  283.8 0.0 all-reduce.6.cloned.1.call-update
  283.8 0.0 copy-done.1
  283.8 1.0 copy.9
  284.8 281.0 %all-reduce.8.cloned.1.call-done = f32[672,672]{1,0:T(8,128)} async-done(((f32[672,672]{1,0:T(8,128)}), f32[672,672]{1,0:T(8,128)}) %all-reduce.8.cloned.1.call-update) | async-done | bytes 1806352 | tf_op jit(solution)/shard_map/psum | solution.py:30
  565.8 3.0 broadcast_multiply_fusion
  568.8 64.6 %all-reduce.6.cloned.1.call-done = f32[672,672]{1,0:T(8,128)} async-done(((f32[672,672]{1,0:T(8,128)}), f32[672,672]{1,0:T(8,128)}) %all-reduce.6.cloned.1.call-update) | async-done | bytes 1806352 | tf_op jit(solution)/shard_map/psum | solution.py:17
  633.4 1.9 dynamic-slice_multiply_fusion
Async XLA Ops:
  8.0 0.9 copy-start
  8.0 67.8 %reduce-scatter.2.cloned.1.call-start = ((), (), s32[]{:S(2)}) async-start(), calls=%async_computation.4 | async-start | bytes 1966080 | tf_op jit(solution)/shard_map/reduce_scatter | solution.py:20
  13.2 270.6 %all-reduce.4.cloned.1.call-start = ((), (), s32[]{:S(2)}) async-start(), calls=%async_computation.2 | async-start | bytes 4128768 | tf_op jit(solution)/shard_map/psum | solution.py:16
  75.6 490.2 %all-reduce.8.cloned.1.call-start = ((), (), s32[]{:S(2)}) async-start(), calls=%async_computation.5 | async-start | bytes 4128768 | tf_op jit(solution)/shard_map/psum | solution.py:30
  80.1 203.7 %copy-start.1 = (f32[32,4,672]{2,0,1:T(8,128)S(1)}, f32[32,4,672]{2,0,1:T(8,128)}, u32[]{:S(2)}) copy-start(f32[32,4,672]{2,0,1:T(8,128)} %reduce-scatter.2.cloned.1.call-done) | copy-start | bytes 1032196
  80.2 553.2 %all-reduce.6.cloned.1.call-start = ((), (), s32[]{:S(2)}) async-start(), calls=%async_computation.3 | async-start | bytes 4128768 | tf_op jit(solution)/shard_map/psum | solution.py:17
Sparse Core Ops, SparseCore 0:
  13.3 54.6 reduce-scatter.1
Sparse Core Ops, SparseCore 1:
  75.7 208.0 all-reduce.3
  289.1 276.6 all-reduce.7
  568.2 65.1 all-reduce.5
